TPU v7x, 256 devices: a whole 4x4x8 slice. The times are simulated.
256 devices in a mesh: req: 64 (over y, z, core), tp: 4 (over x).
Axes of the slice: x: 4, y: 4, z: 8, core: 2. Of those that a mesh axis runs over, the one named last changes fastest.
Arguments:
- patches: bfloat16 [16384, 1280], P('req'), may hold values from -6 to 6
- half_grid: int32 [64, 2], P('req'), may hold values from 6 to 8
- text_embed: bfloat16 [12288, 1280], P('req'), may hold values from -6 to 6
- dest_dev: int32 [4096], P('req'), may hold values from 0 to 63, as said below
- dest_pos: int32 [4096], P('req'), may hold values from 0 to 191, as said below
- text_len: int32 [64], P('req'), may hold values from 1 to 128, as said below
- enc_qkv: bfloat16 [1280, 3840], P('req', 'tp')
- enc_out_t: bfloat16 [1280, 1280], P('req', 'tp'), may hold values from -0.15625 to 0.15625
- enc_up: bfloat16 [1280, 5120], P('req', 'tp'), may hold values from -0.15625 to 0.15625
- enc_down_t: bfloat16 [1280, 5120], P('req', 'tp'), may hold values from -0.078125 to 0.078125
- merge_t: bfloat16 [1280, 5120], P('req', 'tp'), may hold values from -0.078125 to 0.078125
- dec_qkv: bfloat16 [1280, 3840], P('req', 'tp')
- dec_out_t: bfloat16 [1280, 1280], P('req', 'tp'), may hold values from -0.15625 to 0.15625
- dec_up: bfloat16 [1280, 5120], P('req', 'tp'), may hold values from -0.15625 to 0.15625
- dec_down_t: bfloat16 [1280, 5120], P('req', 'tp'), may hold values from -0.078125 to 0.078125
Outputs:
- decoded: bfloat16 [12288, 1280], P('req')
Inputs may be any that keep to these rules, and one draw needn't show every extreme that they name: `dest_dev`: the slots of one device go in runs to destination devices; at most 2 slots of one device name one destination device, exactly 2 for some pairs; every device is named by exactly 64 slots in all. `dest_pos`: positions named for one destination device are distinct and below 64 plus its text_len. `text_len`: some request has exactly 128.
All inputs are finite; a program needn't handle non-finite values.
Results may differ from a plain program's by a relative error of at most 0.024.
Values may be sent and summed in bfloat16 or wider, within the bound.
A program may use at most 64 MiB of HBM per device.

v0:
```python
import jax
import jax.numpy as jnp
from jax import lax
from jax.sharding import PartitionSpec as P

HEAD_DIM = 80
GRID = 16
EPS = 1e-06


def for_sending(shard):

    def short(part):
        return part.astype(jnp.bfloat16) if part.dtype == jnp.float32 else part

    return jax.tree.map(short, shard)


def normalize(stream):
    values_f = stream.astype(jnp.float32)
    center = values_f - jnp.mean(values_f, axis=-1, keepdims=True)
    spread = jnp.mean(center * center, axis=-1, keepdims=True)
    return (center * lax.rsqrt(spread + EPS)).astype(jnp.bfloat16)


def fetch_weights(weights):
    return jax.tree.map(
        lambda part, own: part.astype(own.dtype),
        lax.all_gather(for_sending(weights), "req", axis=0, tiled=True),
        weights,
    )


def tensor_total(partial_value):
    return lax.psum(partial_value.astype(jnp.bfloat16), "tp").astype(jnp.float32)


def attention(normed, w_qkv, w_out_t, allowed, sample_count):
    total_rows = normed.shape[0]
    length = total_rows // sample_count
    projected = jnp.dot(normed, w_qkv, preferred_element_type=jnp.float32).astype(jnp.bfloat16)
    projected = projected.reshape(sample_count, length, -1, 3, HEAD_DIM)
    queries = projected[:, :, :, 0]
    key_part = projected[:, :, :, 1]
    value_part = projected[:, :, :, 2]
    scores = jnp.einsum(
        "bqhd,bkhd->bhqk", queries, key_part, preferred_element_type=jnp.float32
    ) * HEAD_DIM ** (-0.5)
    scores = jnp.where(allowed, scores, -1e30)
    highest = jnp.max(scores, axis=-1, keepdims=True)
    exponent = jnp.exp(scores - highest)
    weights_soft = (exponent / jnp.sum(exponent, axis=-1, keepdims=True)).astype(jnp.bfloat16)
    heads_out = jnp.einsum(
        "bhqk,bkhd->bqhd", weights_soft, value_part, preferred_element_type=jnp.float32
    )
    heads_out = heads_out.astype(jnp.bfloat16).reshape(total_rows, -1)
    return lax.dot_general(
        heads_out, w_out_t, (((1,), (1,)), ((), ())), preferred_element_type=jnp.float32
    )


def feed_forward(normed, w_up, w_down_t):
    hidden = jax.nn.gelu(
        jnp.dot(normed, w_up, preferred_element_type=jnp.float32), approximate=False
    )
    hidden = hidden.astype(jnp.bfloat16)
    return lax.dot_general(
        hidden, w_down_t, (((1,), (1,)), ((), ())), preferred_element_type=jnp.float32
    )


def transformer_layer(stream, weights, allowed, sample_count):
    w_qkv, w_out_t, w_up, w_down_t = weights
    attended = attention(normalize(stream), w_qkv, w_out_t, allowed, sample_count)
    middle = (stream.astype(jnp.float32) + tensor_total(attended)).astype(jnp.bfloat16)
    result_rows = middle.astype(jnp.float32) + tensor_total(
        feed_forward(normalize(middle), w_up, w_down_t)
    )
    result_rows = result_rows.astype(jnp.bfloat16)
    return result_rows


def on_device(
    patches,
    half_grid,
    text_embed,
    dest_dev,
    dest_pos,
    text_len,
    enc_qkv,
    enc_out_t,
    enc_up,
    enc_down_t,
    merge_t,
    dec_qkv,
    dec_out_t,
    dec_up,
    dec_down_t,
):
    image_count = half_grid.shape[0]
    model_width = patches.shape[1]
    per_image = GRID * GRID
    patch_index = jnp.arange(per_image, dtype=jnp.int32)
    key_valid = ((patch_index // GRID)[None, :] < 2 * half_grid[:, 0:1]) & (
        (patch_index % GRID)[None, :] < 2 * half_grid[:, 1:2]
    )
    enc_weights = fetch_weights((enc_qkv, enc_out_t, enc_up, enc_down_t))
    encoded = transformer_layer(patches, enc_weights, key_valid[:, None, None, :], image_count)
    merge_local, qkv_dec, out_dec, up_dec, down_dec = fetch_weights(
        (merge_t, dec_qkv, dec_out_t, dec_up, dec_down_t)
    )
    half_side = GRID // 2
    blocks = encoded.reshape(image_count, half_side, 2, half_side, 2, model_width).transpose(
        0, 1, 3, 2, 4, 5
    )
    blocks = blocks.reshape(image_count * half_side * half_side, 4 * model_width)
    span_width = merge_local.shape[1]
    feature_part = lax.dynamic_slice_in_dim(
        blocks, lax.axis_index("tp") * span_width, span_width, 1
    )
    merge_partial = lax.dot_general(
        feature_part, merge_local, (((1,), (1,)), ((), ())), preferred_element_type=jnp.float32
    )
    merged = tensor_total(merge_partial).astype(jnp.bfloat16)
    slot_count = merged.shape[0]
    senders = lax.axis_size("req")
    even_share = slot_count // senders
    capacity = even_share + max(even_share // 2, 1)
    cell_index = jnp.arange(half_side * half_side, dtype=jnp.int32)
    slot_valid = ((cell_index // half_side)[None, :] < half_grid[:, 0:1]) & (
        (cell_index % half_side)[None, :] < half_grid[:, 1:2]
    )
    slot_valid = slot_valid.reshape(slot_count)
    one_hot = (dest_dev[:, None] == jnp.arange(senders, dtype=jnp.int32)[None, :]).astype(jnp.int32)
    earlier = jnp.cumsum(one_hot, axis=0) - one_hot
    slot_rank = jnp.sum(earlier * one_hot, axis=1)
    outgoing = (
        jnp.zeros((senders, capacity, model_width), jnp.bfloat16)
        .at[dest_dev, slot_rank]
        .set(merged)
    )
    out_pos = (
        jnp.full((senders, capacity), -1, jnp.int32)
        .at[dest_dev, slot_rank]
        .set(jnp.where(slot_valid, dest_pos, -1))
    )
    incoming, in_pos = (
        lax.all_to_all(outgoing, "req", split_axis=0, concat_axis=0, tiled=True),
        lax.all_to_all(out_pos, "req", split_axis=0, concat_axis=0, tiled=True),
    )
    seq_len = text_embed.shape[0]
    target = jnp.where(in_pos >= 0, in_pos, seq_len).astype(jnp.int32).reshape(-1)
    dec_input = text_embed.at[target].set(incoming.reshape(-1, model_width), mode="drop")
    positions = jnp.arange(seq_len, dtype=jnp.int32)
    causal = (positions[:, None] >= positions[None, :])[None, None]
    decoded = transformer_layer(dec_input, (qkv_dec, out_dec, up_dec, down_dec), causal, 1)
    keep_mask = positions < slot_count + text_len[0]
    return jnp.where(keep_mask[:, None], decoded, jnp.zeros_like(decoded))


def solution(mesh):
    return jax.shard_map(
        on_device,
        mesh=mesh,
        in_specs=(
            P("req", None),
            P("req", None),
            P("req", None),
            P("req"),
            P("req"),
            P("req"),
            P("req", "tp"),
            P("req", "tp"),
            P("req", "tp"),
            P("req", "tp"),
            P("req", "tp"),
            P("req", "tp"),
            P("req", "tp"),
            P("req", "tp"),
            P("req", "tp"),
        ),
        out_specs=P("req", None),
        check_vma=False,
    )
```

profile of v0, /device:TPU:8, one launch (start us, length us, event | category | flops | bytes accessed | tf_op | source)
XLA Modules:
  0.0 852.3 jit_solution(17187715245024345156)
XLA Ops:
  6.5 0.7 all-gather.17.cloned.1.call-update
  7.3 1.4 fusion.214
  10.0 53.3 %all-gather.1 = bf16[64,20,320]{2,1,0:T(8,128)(2,1)S(1)} all-gather(bf16[1,20,320]{2,1,0:T(8,128)(2,1)} %bitcast.120), channel_id=1, replica_groups=mesh['req'=64,'tp'=4] {'req'}, dimensions={0}, use_global_device_ids=true | all-gather | bytes 832000 | tf_op jit(solution)/shard_map/all_gather | solution.py:29
  64.9 25.2 %all-gather.17.cloned.1.call-done = bf16[64,20,960]{2,1,0:T(8,128)(2,1)} async-done(((bf16[1,20,960]{2,1,0:T(8,128)(2,1)}), bf16[64,20,960]{2,1,0:T(8,128)(2,1)}) %all-gather.17.cloned.1.call-update) | async-done | bytes 2457616 | tf_op jit(solution)/shard_map/all_gather | solution.py:29
  90.1 5.5 reshape.277
  95.6 2.9 convolution_convert_fusion.5
  99.8 1.4 convolution_convert_fusion
  103.2 45.6 %all-reduce.6.cloned.1.call-done = bf16[256,1280]{1,0:T(8,128)(2,1)} async-done(((bf16[256,1280]{1,0:T(8,128)(2,1)}), bf16[256,1280]{1,0:T(8,128)(2,1)}) %all-reduce.6.cloned.1.call-update) | async-done | bytes 655376 | tf_op jit(solution)/shard_map/psum | solution.py:35
  148.8 1.4 convert_reduce_fusion
  150.5 79.6 %all-gather.19.cloned.1.call-done = bf16[64,20,1280]{2,1,0:T(8,128)(2,1)} async-done(((bf16[1,20,1280]{2,1,0:T(8,128)(2,1)}), bf16[64,20,1280]{2,1,0:T(8,128)(2,1)}) %all-gather.19.cloned.1.call-update) | async-done | bytes 3276816 | tf_op jit(solution)/shard_map/all_gather | solution.py:29
  230.1 6.1 reshape.281
  236.2 72.5 %all-gather.21.cloned.1.call-done = bf16[64,20,1280]{2,1,0:T(8,128)(2,1)} async-done(((bf16[1,20,1280]{2,1,0:T(8,128)(2,1)}), bf16[64,20,1280]{2,1,0:T(8,128)(2,1)}) %all-gather.21.cloned.1.call-update) | async-done | bytes 3276816 | tf_op jit(solution)/shard_map/all_gather | solution.py:29
  308.7 6.1 reshape.283
  314.8 8.2 convolution_convert_fusion.1
  323.3 64.0 %all-gather.23.cloned.1.call-done = bf16[64,20,1280]{2,1,0:T(8,128)(2,1)} async-done(((bf16[1,20,1280]{2,1,0:T(8,128)(2,1)}), bf16[64,20,1280]{2,1,0:T(8,128)(2,1)}) %all-gather.23.cloned.1.call-update) | async-done | bytes 3276816 | tf_op jit(solution)/shard_map/all_gather | solution.py:29
  387.3 4.6 reshape.285
  391.9 44.6 %all-reduce.8.cloned.1.call-done = bf16[256,1280]{1,0:T(8,128)(2,1)} async-done(((bf16[256,1280]{1,0:T(8,128)(2,1)}), bf16[256,1280]{1,0:T(8,128)(2,1)}) %all-reduce.8.cloned.1.call-update) | async-done | bytes 655376 | tf_op jit(solution)/shard_map/psum | solution.py:35
  436.5 2.3 fusion.15
  438.8 2.6 reshape.248
  441.4 2.4 copy.56
  443.8 2.9 reshape.249
  446.7 2.7 convolution_convert_fusion.4
  449.5 0.7 all-gather.25.cloned.1.call-update
  450.3 0.7 all-gather.27.cloned.1.call-update
  451.9 1.3 and_select_fusion.2
  453.2 3.5 scatter_fusion
  456.7 0.7 copy.36
  457.4 10.6 %all-to-all-start = ((s32[64,1,2]{2,1,0:T(1,128)}), s32[64,1,2]{2,1,0:T(1,128)S(1)}, u32[]{:S(2)}, u32[]{:S(2)}) async-start(s32[64,1,2]{2,1,0:T(1,128)} %copy.36), calls=%async_computation | async-start | bytes 65536 | tf_op jit(solution)/shard_map/all_to_all | solution.py:149
  468.0 28.8 %all-reduce.10.cloned.1.call-done = bf16[64,1280]{1,0:T(8,128)(2,1)} async-done(((bf16[64,1280]{1,0:T(8,128)(2,1)}), bf16[64,1280]{1,0:T(8,128)(2,1)}) %all-reduce.10.cloned.1.call-update) | async-done | bytes 163856 | tf_op jit(solution)/shard_map/psum | solution.py:35
  496.8 0.9 broadcast_in_dim.47
  497.7 10.0 %scatter_fusion.1 = bf16[64,2,1280]{2,1,0:T(2,128)(2,1)} fusion(bf16[64,2,1280]{2,1,0:T(2,128)(2,1)} %broadcast_in_dim.47, s32[64]{0:T(128)S(1)} %fusion.146, bf16[64,1280]{1,0:T(8,128)(2,1)} %all-reduce.10.cloned.1.call-done), kind=kCustom, calls=%fused_computation.1 | custom fusion | bytes 492032 | tf_op jit(solution)/shard_map/scatter | solution.py:140
  507.7 10.6 %all-to-all-start.1 = ((bf16[64,2,1280]{2,1,0:T(2,128)(2,1)}), bf16[64,2,1280]{2,1,0:T(2,128)(2,1)S(1)}, u32[]{:S(2)}, u32[]{:S(2)}) async-start(bf16[64,2,1280]{2,1,0:T(2,128)(2,1)} %scatter_fusion.1), calls=%async_computation.1 | async-start | bytes 655360 | tf_op jit(solution)/shard_map/all_to_all | solution.py:148
  518.4 54.4 %all-gather.6 = bf16[64,20,320]{2,1,0:T(8,128)(2,1)S(1)} all-gather(bf16[1,20,320]{2,1,0:T(8,128)(2,1)S(1)} %bitcast.121), channel_id=1, replica_groups=mesh['req'=64,'tp'=4] {'req'}, dimensions={0}, use_global_device_ids=true | all-gather | bytes 832000 | tf_op jit(solution)/shard_map/all_gather | solution.py:29
  574.5 4.0 all-gather.25.cloned.1.call-done
  578.5 5.5 reshape.287
  584.2 0.9 copy-done
  585.1 1.6 scatter_fusion.2
  587.1 2.5 convolution_convert_fusion.6
  590.9 1.3 convolution_convert_fusion.3
  592.3 65.9 %all-gather.27.cloned.1.call-done = bf16[64,20,1280]{2,1,0:T(8,128)(2,1)} async-done(((bf16[1,20,1280]{2,1,0:T(8,128)(2,1)}), bf16[64,20,1280]{2,1,0:T(8,128)(2,1)}) %all-gather.27.cloned.1.call-update) | async-done | bytes 3276816 | tf_op jit(solution)/shard_map/all_gather | solution.py:29
  658.2 6.1 reshape.291
  664.3 72.8 %all-gather.29.cloned.1.call-done = bf16[64,20,1280]{2,1,0:T(8,128)(2,1)} async-done(((bf16[1,20,1280]{2,1,0:T(8,128)(2,1)}), bf16[64,20,1280]{2,1,0:T(8,128)(2,1)}) %all-gather.29.cloned.1.call-update) | async-done | bytes 3276816 | tf_op jit(solution)/shard_map/all_gather | solution.py:29
  737.1 6.1 reshape.293
  743.2 42.6 %all-reduce.12.cloned.1.call-done = bf16[192,1280]{1,0:T(8,128)(2,1)} async-done(((bf16[192,1280]{1,0:T(8,128)(2,1)}), bf16[192,1280]{1,0:T(8,128)(2,1)}) %all-reduce.12.cloned.1.call-update) | async-done | bytes 491536 | tf_op jit(solution)/shard_map/psum | solution.py:35
  785.8 1.3 convert_reduce_fusion.2
  787.4 7.4 convolution_convert_fusion.2
  795.5 48.0 %all-reduce.14.cloned.1.call-done = bf16[192,1280]{1,0:T(8,128)(2,1)} async-done(((bf16[192,1280]{1,0:T(8,128)(2,1)}), bf16[192,1280]{1,0:T(8,128)(2,1)}) %all-reduce.14.cloned.1.call-update) | async-done | bytes 491536 | tf_op jit(solution)/shard_map/psum | solution.py:35
  843.5 2.0 fusion.93
  (70 shorter events, 10.4 us)
Async XLA Ops:
  6.5 83.6 %all-gather.17.cloned.1.call-start = ((), (), s32[]{:S(2)}) async-start(), calls=%async_computation.7 | async-start | bytes 3194880 | tf_op jit(solution)/shard_map/all_gather | solution.py:29
  7.3 141.5 %all-reduce.6.cloned.1.call-start = ((), (), s32[]{:S(2)}) async-start(), calls=%async_computation.2 | async-start | bytes 1310720 | tf_op jit(solution)/shard_map/psum | solution.py:35
  63.3 1.1 copy-start.1
  101.3 128.8 %all-gather.19.cloned.1.call-start = ((), (), s32[]{:S(2)}) async-start(), calls=%async_computation.8 | async-start | bytes 3993600 | tf_op jit(solution)/shard_map/all_gather | solution.py:29
  102.0 206.7 %all-gather.21.cloned.1.call-start = ((), (), s32[]{:S(2)}) async-start(), calls=%async_computation.9 | async-start | bytes 3993600 | tf_op jit(solution)/shard_map/all_gather | solution.py:29
  102.6 284.7 %all-gather.23.cloned.1.call-start = ((), (), s32[]{:S(2)}) async-start(), calls=%async_computation.10 | async-start | bytes 3993600 | tf_op jit(solution)/shard_map/all_gather | solution.py:29
  103.2 333.4 %all-reduce.8.cloned.1.call-start = ((), (), s32[]{:S(2)}) async-start(), calls=%async_computation.3 | async-start | bytes 1310720 | tf_op jit(solution)/shard_map/psum | solution.py:35
  150.1 164.6 %copy-start.2 = (bf16[256,1280]{1,0:T(8,128)(2,1)}, bf16[256,1280]{1,0:T(8,128)(2,1)S(1)}, u32[]{:S(2)}) copy-start(bf16[256,1280]{1,0:T(8,128)(2,1)S(1)} %get-tuple-element.8) | copy-start | bytes 1966084
  323.0 173.8 %all-reduce.10.cloned.1.call-start = ((), (), s32[]{:S(2)}) async-start(), calls=%async_computation.4 | async-start | bytes 327680 | tf_op jit(solution)/shard_map/psum | solution.py:35
  446.7 4.8 copy-start.4
  446.7 5.2 copy-start.5
  449.5 129.1 %all-gather.25.cloned.1.call-start = ((), (), s32[]{:S(2)}) async-start(), calls=%async_computation.11 | async-start | bytes 3194880 | tf_op jit(solution)/shard_map/all_gather | solution.py:29
  450.2 208.0 %all-gather.27.cloned.1.call-start = ((), (), s32[]{:S(2)}) async-start(), calls=%async_computation.12 | async-start | bytes 3993600 | tf_op jit(solution)/shard_map/all_gather | solution.py:29
  451.0 286.2 %all-gather.29.cloned.1.call-start = ((), (), s32[]{:S(2)}) async-start(), calls=%async_computation.13 | async-start | bytes 3993600 | tf_op jit(solution)/shard_map/all_gather | solution.py:29
  457.4 50.3 %all-to-all-start = ((s32[64,1,2]{2,1,0:T(1,128)}), s32[64,1,2]{2,1,0:T(1,128)S(1)}, u32[]{:S(2)}, u32[]{:S(2)}) async-start(s32[64,1,2]{2,1,0:T(1,128)} %copy.36), calls=%async_computation | async-start | bytes 65536 | tf_op jit(solution)/shard_map/all_to_all | solution.py:149
  497.7 20.6 %copy-start.3 = (bf16[20,320]{1,0:T(8,128)(2,1)S(1)}, bf16[20,320]{1,0:T(8,128)(2,1)}, u32[]{:S(2)}) copy-start(bf16[20,320]{1,0:T(8,128)(2,1)} %param.27) | copy-start | bytes 38404
  507.7 76.3 %all-to-all-start.1 = ((bf16[64,2,1280]{2,1,0:T(2,128)(2,1)}), bf16[64,2,1280]{2,1,0:T(2,128)(2,1)S(1)}, u32[]{:S(2)}, u32[]{:S(2)}) async-start(bf16[64,2,1280]{2,1,0:T(2,128)(2,1)} %scatter_fusion.1), calls=%async_computation.1 | async-start | bytes 655360 | tf_op jit(solution)/shard_map/all_to_all | solution.py:148
  518.3 267.5 %all-reduce.12.cloned.1.call-start = ((), (), s32[]{:S(2)}) async-start(), calls=%async_computation.5 | async-start | bytes 983040 | tf_op jit(solution)/shard_map/psum | solution.py:35
  584.0 1.0 copy-start
  592.3 251.2 %all-reduce.14.cloned.1.call-start = ((), (), s32[]{:S(2)}) async-start(), calls=%async_computation.6 | async-start | bytes 983040 | tf_op jit(solution)/shard_map/psum | solution.py:35
Sparse Core Ops, SparseCore 0:
  10.1 79.9 all-gather.16
  101.4 47.3 all-reduce.5
  151.5 78.5 all-gather.18
  232.6 76.0 all-gather.20
  311.2 76.0 all-gather.22
  389.5 47.0 all-reduce.7
  449.6 47.2 all-reduce.9
  500.0 78.5 all-gather.24
  581.6 76.5 all-gather.26
  661.1 76.0 all-gather.28
  739.6 46.1 all-reduce.11
  794.9 48.4 all-reduce.13
where the time goes:
time: 854 us; the launch traced here: 852 us
  waiting for transfers between devices  598 us (70%)
  blocking collectives  108 us (13%)
  local copies, waits for them, and re-layouts  69.4 us (8%)
  matrix products  28.9 us (3%)
  starting transfers between devices  21.7 us (3%)
  between operations  15.7 us (2%)
  other arithmetic  10.7 us (1%)
    all_gather x7, waiting for transfers between devices, fetch_weights(): lax.all_gather(for_sending(weights), 'req', axis=0, tiled=True)  384 us
    psum x5, waiting for transfers between devices, tensor_total(): lax.psum(partial_value.astype(jnp.bfloat16), 'tp').astype(jnp.float32)  210 us
    all_gather x2, blocking collectives, fetch_weights(): lax.all_gather(for_sending(weights), 'req', axis=0, tiled=True)  108 us
    unnamed x21, local copies, waits for them, and re-layouts  42.5 us
  transfers between devices with their start and end apart: 14, of which 12 were waited for; matrix products, arithmetic and copies ran while one was open for 8% of the time, Pallas kernels for 0%

commit v1 on v0

--- a/solution.py
+++ b/solution.py
@@ -32,7 +32,7 @@
 
 
 def tensor_total(partial_value):
-    return lax.psum(partial_value.astype(jnp.bfloat16), "tp").astype(jnp.float32)
+    return jnp.sum(lax.all_gather(partial_value.astype(jnp.bfloat16), "tp"), 0).astype(jnp.float32)
 
 
 def attention(normed, w_qkv, w_out_t, allowed, sample_count):

time: 854 us -> 730 us (0.85)
  waiting for transfers between devices: 598 us -> 453 us
  blocking collectives: 108 us -> 123 us
    psum x5 -> x0, waiting for transfers between devices: 210 us -> none  [tensor_total(): lax.psum(partial_value.astype(jnp.bfloat16), 'tp').astype(jnp.float32)]
    all_gather x0 -> x4, waiting for transfers between devices: none -> 123 us  [tensor_total(): lax.all_gather(partial_value.astype(jnp.bfloat16), 'tp')]
    all_gather x7, waiting for transfers between devices: 384 us -> 325 us  [fetch_weights(): lax.all_gather(for_sending(weights), 'req', axis=0, tiled=True)]
    all_gather x0 -> x1, blocking collectives: none -> 13.9 us  [tensor_total(): lax.all_gather(partial_value.astype(jnp.bfloat16), 'tp')]
    reduce_sum x0 -> x5, other arithmetic: none -> 9.77 us  [tensor_total(): jnp.sum(lax.all_gather(partial_value.astype(jnp.bfloat16), 'tp'), 0)]
  transfers between devices with their start and end apart: 14 -> 13, of which waited for: 12 -> 10; matrix products, arithmetic and copies ran while one was open for 8% -> 14% of each run, Pallas kernels for 0% -> 0%
where the time goes in v1:
time: 730 us; the launch traced here: 728 us
  waiting for transfers between devices  453 us (62%)
  blocking collectives  123 us (17%)
  local copies, waits for them, and re-layouts  69.1 us (9%)
  matrix products  28.2 us (4%)
  starting transfers between devices  21.9 us (3%)
  other arithmetic  17.4 us (2%)
  between operations  15.4 us (2%)
    all_gather x7, waiting for transfers between devices, fetch_weights(): lax.all_gather(for_sending(weights), 'req', axis=0, tiled=True)  325 us
    all_gather x4, waiting for transfers between devices, tensor_total(): lax.all_gather(partial_value.astype(jnp.bfloat16), 'tp')  123 us
    all_gather x2, blocking collectives, fetch_weights(): lax.all_gather(for_sending(weights), 'req', axis=0, tiled=True)  109 us
    unnamed x21, local copies, waits for them, and re-layouts  42.6 us
    dot_general x2, matrix products, feed_forward(): lax.dot_general(hidden, w_down_t, (((1,), (1,)), ((), ())), preferred_ele...  15.7 us
  transfers between devices with their start and end apart: 13, of which 10 were waited for; matrix products, arithmetic and copies ran while one was open for 14% of the time, Pallas kernels for 0%

profile of v1, /device:TPU:8, one launch (start us, length us, event | category | flops | bytes accessed | tf_op | source)
XLA Modules:
  0.0 727.5 jit_solution(6058165702033979612)
XLA Ops:
  6.5 0.7 all-gather.34.cloned.1.call-update
  8.8 1.3 fusion.214
  11.4 53.4 %all-gather.6 = bf16[64,20,320]{2,1,0:T(8,128)(2,1)S(1)} all-gather(bf16[1,20,320]{2,1,0:T(8,128)(2,1)} %bitcast.130), channel_id=1, replica_groups=mesh['req'=64,'tp'=4] {'req'}, dimensions={0}, use_global_device_ids=true | all-gather | bytes 832000 | tf_op jit(solution)/shard_map/all_gather | solution.py:29
  66.4 23.8 %all-gather.34.cloned.1.call-done = bf16[64,20,960]{2,1,0:T(8,128)(2,1)} async-done(((bf16[1,20,960]{2,1,0:T(8,128)(2,1)}), bf16[64,20,960]{2,1,0:T(8,128)(2,1)}) %all-gather.34.cloned.1.call-update) | async-done | bytes 2457616 | tf_op jit(solution)/shard_map/all_gather | solution.py:29
  90.2 5.5 reshape.282
  95.7 2.9 convolution_convert_fusion.5
  99.9 1.4 convolution_convert_fusion
  102.1 67.1 %all-gather.36.cloned.1.call-done = bf16[64,20,1280]{2,1,0:T(8,128)(2,1)} async-done(((bf16[1,20,1280]{2,1,0:T(8,128)(2,1)}), bf16[64,20,1280]{2,1,0:T(8,128)(2,1)}) %all-gather.36.cloned.1.call-update) | async-done | bytes 3276816 | tf_op jit(solution)/shard_map/all_gather | solution.py:29
  169.2 6.1 reshape.286
  175.4 72.6 %all-gather.38.cloned.1.call-done = bf16[64,20,1280]{2,1,0:T(8,128)(2,1)} async-done(((bf16[1,20,1280]{2,1,0:T(8,128)(2,1)}), bf16[64,20,1280]{2,1,0:T(8,128)(2,1)}) %all-gather.38.cloned.1.call-update) | async-done | bytes 3276816 | tf_op jit(solution)/shard_map/all_gather | solution.py:29
  248.0 6.1 reshape.288
  254.1 31.6 %all-gather.26.cloned.1.call-done = bf16[1024,1280]{1,0:T(8,128)(2,1)} async-done(((bf16[256,1280]{1,0:T(8,128)(2,1)}), bf16[1024,1280]{1,0:T(8,128)(2,1)}) %all-gather.26.cloned.1.call-update) | async-done | bytes 2621456 | tf_op jit(solution)/shard_map/all_gather | solution.py:35
  285.7 2.4 reduce_sum.166
  288.8 8.3 %convolution_convert_fusion.1 = bf16[256,1280]{1,0:T(8,128)(2,1)} fusion(bf16[1280,1280]{1,0:T(8,128)(2,1)} %reshape.288, bf16[1280,1280]{1,0:T(8,128)(2,1)} %reshape.286, bf16[256,1280]{1,0:T(8,128)(2,1)S(1)} %get-tuple-element.8, f32[256]{0:T(256)S(1)} %add_rsqrt_fusion.2, f32[256]{0:T(256)S(1)} %broadcast_multiply_fusion.2), kind=kOutput, calls=%fused_computation.6 | convolution fusion | flops 1700659200 | bytes 7866368 | tf_op jit(solution)/shard_map/dot_general | solution.py:67
  299.7 1.3 and_select_fusion.2
  301.0 3.5 scatter_fusion
  304.5 0.7 copy.36
  305.2 10.6 %all-to-all-start = ((s32[64,1,2]{2,1,0:T(1,128)}), s32[64,1,2]{2,1,0:T(1,128)S(1)}, u32[]{:S(2)}, u32[]{:S(2)}) async-start(s32[64,1,2]{2,1,0:T(1,128)} %copy.36), calls=%async_computation | async-start | bytes 65536 | tf_op jit(solution)/shard_map/all_to_all | solution.py:149
  315.8 50.3 %all-gather.40.cloned.1.call-done = bf16[64,20,1280]{2,1,0:T(8,128)(2,1)} async-done(((bf16[1,20,1280]{2,1,0:T(8,128)(2,1)}), bf16[64,20,1280]{2,1,0:T(8,128)(2,1)}) %all-gather.40.cloned.1.call-update) | async-done | bytes 3276816 | tf_op jit(solution)/shard_map/all_gather | solution.py:29
  366.1 4.6 reshape.290
  370.8 33.1 %all-gather.28.cloned.1.call-done = bf16[1024,1280]{1,0:T(8,128)(2,1)} async-done(((bf16[256,1280]{1,0:T(8,128)(2,1)}), bf16[1024,1280]{1,0:T(8,128)(2,1)}) %all-gather.28.cloned.1.call-update) | async-done | bytes 2621456 | tf_op jit(solution)/shard_map/all_gather | solution.py:35
  403.9 3.2 reduce_sum.169
  407.1 2.3 fusion.15
  409.4 2.7 reshape.248
  412.0 2.4 copy.56
  414.4 2.9 reshape.249
  417.4 2.0 convolution_convert_fusion.4
  419.4 13.9 %all-gather.2 = bf16[256,1280]{1,0:T(8,128)(2,1)S(1)} all-gather(bf16[64,1280]{1,0:T(8,128)(2,1)S(1)} %convolution_convert_fusion.4), channel_id=4, replica_groups=mesh['req'=64,'tp'=4] {'tp'}, dimensions={0}, use_global_device_ids=true | all-gather | bytes 819200 | tf_op jit(solution)/shard_map/all_gather | solution.py:35
  433.4 0.9 broadcast_in_dim.47
  434.3 9.6 %scatter_fusion.1 = bf16[64,2,1280]{2,1,0:T(2,128)(2,1)} fusion(bf16[64,2,1280]{2,1,0:T(2,128)(2,1)} %broadcast_in_dim.47, s32[64]{0:T(128)S(1)} %fusion.146, bf16[64,1280]{1,0:T(8,128)(2,1)S(1)} %reduce_sum.170), kind=kCustom, calls=%fused_computation.1 | custom fusion | bytes 492032 | tf_op jit(solution)/shard_map/scatter | solution.py:140
  443.9 10.5 %all-to-all-start.1 = ((bf16[64,2,1280]{2,1,0:T(2,128)(2,1)}), bf16[64,2,1280]{2,1,0:T(2,128)(2,1)S(1)}, u32[]{:S(2)}, u32[]{:S(2)}) async-start(bf16[64,2,1280]{2,1,0:T(2,128)(2,1)} %scatter_fusion.1), calls=%async_computation.1 | async-start | bytes 655360 | tf_op jit(solution)/shard_map/all_to_all | solution.py:148
  454.5 55.6 %all-gather.11 = bf16[64,20,320]{2,1,0:T(8,128)(2,1)S(1)} all-gather(bf16[1,20,320]{2,1,0:T(8,128)(2,1)S(1)} %bitcast.131), channel_id=1, replica_groups=mesh['req'=64,'tp'=4] {'req'}, dimensions={0}, use_global_device_ids=true | all-gather | bytes 832000 | tf_op jit(solution)/shard_map/all_gather | solution.py:29
  511.1 0.7 reduce.16
  511.9 5.6 reshape.292
  517.7 0.9 copy-done
  518.6 1.4 scatter_fusion.2
  520.4 2.5 convolution_convert_fusion.6
  524.2 1.3 convolution_convert_fusion.3
  525.8 38.7 %all-gather.44.cloned.1.call-done = bf16[64,20,1280]{2,1,0:T(8,128)(2,1)} async-done(((bf16[1,20,1280]{2,1,0:T(8,128)(2,1)}), bf16[64,20,1280]{2,1,0:T(8,128)(2,1)}) %all-gather.44.cloned.1.call-update) | async-done | bytes 3276816 | tf_op jit(solution)/shard_map/all_gather | solution.py:29
  564.5 6.1 reshape.296
  570.7 72.6 %all-gather.46.cloned.1.call-done = bf16[64,20,1280]{2,1,0:T(8,128)(2,1)} async-done(((bf16[1,20,1280]{2,1,0:T(8,128)(2,1)}), bf16[64,20,1280]{2,1,0:T(8,128)(2,1)}) %all-gather.46.cloned.1.call-update) | async-done | bytes 3276816 | tf_op jit(solution)/shard_map/all_gather | solution.py:29
  643.3 6.1 reshape.298
  649.4 26.2 %all-gather.30.cloned.1.call-done = bf16[768,1280]{1,0:T(8,128)(2,1)} async-done(((bf16[192,1280]{1,0:T(8,128)(2,1)}), bf16[768,1280]{1,0:T(8,128)(2,1)}) %all-gather.30.cloned.1.call-update) | async-done | bytes 1966096 | tf_op jit(solution)/shard_map/all_gather | solution.py:35
  675.6 2.0 reduce_sum.174
  678.1 7.4 %convolution_convert_fusion.2 = bf16[192,1280]{1,0:T(8,128)(2,1)} fusion(bf16[1280,1280]{1,0:T(8,128)(2,1)} %reshape.298, bf16[1280,1280]{1,0:T(8,128)(2,1)} %reshape.296, bf16[192,1280]{1,0:T(8,128)(2,1)S(1)} %get-tuple-element.6, f32[192]{0:T(256)S(1)} %add_rsqrt_fusion, f32[192]{0:T(256)S(1)} %broadcast_multiply_fusion), kind=kOutput, calls=%fused_computation.7 | convolution fusion | flops 1275494400 | bytes 7538176 | tf_op jit(solution)/shard_map/dot_general | solution.py:67
  686.2 31.8 %all-gather.32.cloned.1.call-done = bf16[768,1280]{1,0:T(8,128)(2,1)} async-done(((bf16[192,1280]{1,0:T(8,128)(2,1)}), bf16[768,1280]{1,0:T(8,128)(2,1)}) %all-gather.32.cloned.1.call-update) | async-done | bytes 1966096 | tf_op jit(solution)/shard_map/all_gather | solution.py:35
  718.0 2.0 reduce_sum.177
  720.1 0.9 fusion.93
  (73 shorter events, 12.4 us)
Async XLA Ops:
  6.5 83.6 %all-gather.34.cloned.1.call-start = ((), (), s32[]{:S(2)}) async-start(), calls=%async_computation.6 | async-start | bytes 3194880 | tf_op jit(solution)/shard_map/all_gather | solution.py:29
  7.3 162.0 %all-gather.36.cloned.1.call-start = ((), (), s32[]{:S(2)}) async-start(), calls=%async_computation.7 | async-start | bytes 3993600 | tf_op jit(solution)/shard_map/all_gather | solution.py:29
  8.0 240.0 %all-gather.38.cloned.1.call-start = ((), (), s32[]{:S(2)}) async-start(), calls=%async_computation.8 | async-start | bytes 3993600 | tf_op jit(solution)/shard_map/all_gather | solution.py:29
  8.7 277.0 %all-gather.26.cloned.1.call-start = ((), (), s32[]{:S(2)}) async-start(), calls=%async_computation.2 | async-start | bytes 3276800 | tf_op jit(solution)/shard_map/all_gather | solution.py:35
  64.8 1.1 copy-start.1
  101.3 264.8 %all-gather.40.cloned.1.call-start = ((), (), s32[]{:S(2)}) async-start(), calls=%async_computation.9 | async-start | bytes 3993600 | tf_op jit(solution)/shard_map/all_gather | solution.py:29
  101.9 302.0 %all-gather.28.cloned.1.call-start = ((), (), s32[]{:S(2)}) async-start(), calls=%async_computation.3 | async-start | bytes 3276800 | tf_op jit(solution)/shard_map/all_gather | solution.py:35
  288.4 8.7 %copy-start.2 = (bf16[256,1280]{1,0:T(8,128)(2,1)}, bf16[256,1280]{1,0:T(8,128)(2,1)S(1)}, u32[]{:S(2)}) copy-start(bf16[256,1280]{1,0:T(8,128)(2,1)S(1)} %get-tuple-element.8) | copy-start | bytes 1966084
  288.8 10.6 %copy-start.4 = (s32[64]{0:T(128)S(1)}, s32[64]{0:T(128)}, u32[]{:S(2)}) copy-start(s32[64]{0:T(128)} %param.18) | copy-start | bytes 772
  288.8 10.9 %copy-start.5 = (s32[64]{0:T(128)S(1)}, s32[64]{0:T(128)}, u32[]{:S(2)}) copy-start(s32[64]{0:T(128)} %param.19) | copy-start | bytes 772
  297.1 214.8 %all-gather.42.cloned.1.call-start = ((), (), s32[]{:S(2)}) async-start(), calls=%async_computation.10 | async-start | bytes 3194880 | tf_op jit(solution)/shard_map/all_gather | solution.py:29
  297.9 266.7 %all-gather.44.cloned.1.call-start = ((), (), s32[]{:S(2)}) async-start(), calls=%async_computation.11 | async-start | bytes 3993600 | tf_op jit(solution)/shard_map/all_gather | solution.py:29
  298.6 344.7 %all-gather.46.cloned.1.call-start = ((), (), s32[]{:S(2)}) async-start(), calls=%async_computation.12 | async-start | bytes 3993600 | tf_op jit(solution)/shard_map/all_gather | solution.py:29
  305.2 138.7 %all-to-all-start = ((s32[64,1,2]{2,1,0:T(1,128)}), s32[64,1,2]{2,1,0:T(1,128)S(1)}, u32[]{:S(2)}, u32[]{:S(2)}) async-start(s32[64,1,2]{2,1,0:T(1,128)} %copy.36), calls=%async_computation | async-start | bytes 65536 | tf_op jit(solution)/shard_map/all_to_all | solution.py:149
  434.3 20.2 %copy-start.3 = (bf16[20,320]{1,0:T(8,128)(2,1)S(1)}, bf16[20,320]{1,0:T(8,128)(2,1)}, u32[]{:S(2)}) copy-start(bf16[20,320]{1,0:T(8,128)(2,1)} %param.27) | copy-start | bytes 38404
  443.9 73.6 %all-to-all-start.1 = ((bf16[64,2,1280]{2,1,0:T(2,128)(2,1)}), bf16[64,2,1280]{2,1,0:T(2,128)(2,1)S(1)}, u32[]{:S(2)}, u32[]{:S(2)}) async-start(bf16[64,2,1280]{2,1,0:T(2,128)(2,1)} %scatter_fusion.1), calls=%async_computation.1 | async-start | bytes 655360 | tf_op jit(solution)/shard_map/all_to_all | solution.py:148
  454.4 221.2 %all-gather.30.cloned.1.call-start = ((), (), s32[]{:S(2)}) async-start(), calls=%async_computation.4 | async-start | bytes 2457600 | tf_op jit(solution)/shard_map/all_gather | solution.py:35
  517.5 1.0 copy-start
  525.5 192.5 %all-gather.32.cloned.1.call-start = ((), (), s32[]{:S(2)}) async-start(), calls=%async_computation.5 | async-start | bytes 2457600 | tf_op jit(solution)/shard_map/all_gather | solution.py:35
Sparse Core Ops, SparseCore 0:
  10.1 80.0 all-gather.33
  92.8 76.3 all-gather.35
  171.9 76.0 all-gather.37
  249.7 36.0 all-gather.25
  288.3 77.8 all-gather.39
  367.8 36.0 all-gather.27
  406.6 78.5 all-gather.41
  487.9 76.6 all-gather.43
  567.2 76.0 all-gather.45
  644.9 30.5 all-gather.29
  685.7 32.2 all-gather.31
